TPU v7x, 512 devices: a whole 4x8x8 slice. The times are simulated.
512 devices in a mesh: leaf: 128 (over z, y, core), rhs: 4 (over x).
Axes of the slice: x: 4, y: 8, z: 8, core: 2. Of those that a mesh axis runs over, the one named last changes fastest.
Arguments:
- potential: float32 [128, 1048576], P('rhs', 'leaf'), may hold values from -6 to 6
- geometry: float32 [4, 1048576], P(None, 'leaf'), as said below
- near_count: int32 [4096], P('leaf'), may hold values from 3 to 12, as said below
- near_offset: int32 [4096, 12], P('leaf'), may hold values from -6 to 6, as said below
- far_offset: int32 [4096, 4], P('leaf'), may hold values from -8 to 8, as said below
- col_basis: bfloat16 [4096, 256, 64], P('leaf'), may hold values from -0.375 to 0.375
- row_basis: bfloat16 [4096, 256, 64], P('leaf'), may hold values from -0.5 to 0.5
- leaf_up: bfloat16 [4096, 64, 64], P('leaf'), may hold values from -0.125 to 0.125
- leaf_down: bfloat16 [4096, 64, 64], P('leaf'), may hold values from -0.75 to 0.75
- leaf_coupling: bfloat16 [4096, 4, 64, 64], P('leaf'), may hold values from -0.375 to 0.375
- up_transfer: bfloat16 [2, 64, 64], replicated, may hold values from -0.5 to 0.5
- down_transfer: bfloat16 [2, 64, 64], replicated, may hold values from -0.75 to 0.75
- sibling_coupling: bfloat16 [2, 64, 64], replicated, may hold values from -0.375 to 0.375
Outputs:
- field: float32 [128, 1048576], P('rhs', 'leaf')
Inputs may be any that keep to these rules, and one draw needn't show every extreme that they name: `geometry`: rows 0 to 2 are panel centroids, row 3 panel areas between 0.005 and 0.05. Each leaf cluster uses slots 0 to near_count - 1; some cluster uses all 12. `near_offset`: slot 0 of every cluster is the cluster itself (offset 0), slot 1 holds a positive offset and slot 2 a negative one; the other slots of a cluster hold distinct nonzero offsets. `far_offset`: every offset has magnitude above 6; the offsets of one cluster are distinct.
All inputs are finite; a program needn't handle non-finite values.
Results may differ from a plain program's by a relative error of at most 0.007.
Values may be sent and summed in bfloat16 or wider, within the bound.
No kernel may reach another device: no remote copies, remote signals or barrier semaphores. Data moves between devices by JAX's collectives and lax.ppermute only.
A program may use at most 64 MiB of HBM per device.

v0:
```python
import math
import jax
import jax.numpy as jnp
from jax import lax
from jax.sharding import PartitionSpec as P

NNEAR = 12
NWIN = 6
FWIN = 8


def with_halo(value, sides, width):
    for axis, dim in sides:
        devices, length = (lax.axis_size(axis), value.shape[dim])
        up = [(i, (i + 1) % devices) for i in range(devices - 1)]
        down = [(j, i) for i, j in up]
        last = lax.slice_in_dim(value, length - width, length, axis=dim)
        first = lax.slice_in_dim(value, 0, width, axis=dim)
        before = lax.ppermute(last, axis, up)
        after = lax.ppermute(first, axis, down)
        value = jnp.concatenate([before, value, after], axis=dim)
    return value


def from_partner(value, axis, apart):
    return lax.ppermute(value, axis, [(i, i ^ 1 << apart) for i in range(lax.axis_size(axis))])


def kernel_entries(target_geometry, source_geometry):
    squared = (target_geometry[0][:, :, None] - source_geometry[0][:, None, :]) ** 2
    squared = squared + (target_geometry[1][:, :, None] - source_geometry[1][:, None, :]) ** 2
    squared = squared + (target_geometry[2][:, :, None] - source_geometry[2][:, None, :]) ** 2
    spread = (target_geometry[3][:, :, None] + source_geometry[3][:, None, :]) / math.pi
    return source_geometry[3][:, None, :] / jnp.sqrt(squared + spread)


def select_side(table, side_bit):
    return lax.dynamic_index_in_dim(table, side_bit, 0, keepdims=False)


def per_device(
    potential,
    geometry,
    near_count,
    near_offset,
    far_offset,
    col_basis,
    row_basis,
    leaf_up,
    leaf_down,
    leaf_coupling,
    up_transfer,
    down_transfer,
    sibling_coupling,
):
    rows_here = potential.shape[0]
    clusters = near_count.shape[0]
    panels = col_basis.shape[1]
    basis_rank = col_basis.shape[2]
    partners_count = far_offset.shape[1]
    column_parts = lax.axis_size("rhs")
    per_part = clusters // column_parts
    first_local = lax.axis_index("rhs") * per_part
    window_width = per_part + 2 * NWIN
    stacked = jnp.concatenate([potential, geometry], axis=0)
    extended = with_halo(stacked, (("leaf", 1),), NWIN * panels)
    wide_rows = extended.shape[1] // panels
    value_rows = extended[:rows_here].astype(jnp.bfloat16)
    sources = lax.all_gather(value_rows, "rhs", axis=0, tiled=True)
    sources = sources.reshape(rows_here * column_parts, wide_rows, panels)
    all_rows = sources.shape[0]
    wide_geometry = extended[rows_here:].reshape(4, wide_rows, panels)
    local_geometry = lax.dynamic_slice_in_dim(wide_geometry, first_local, window_width, 1)
    target_geometry = local_geometry[:, NWIN : NWIN + per_part]
    live_counts = lax.dynamic_slice_in_dim(near_count, first_local, per_part, 0)
    offsets = lax.dynamic_slice_in_dim(near_offset, first_local, per_part, 0)
    own_clusters = NWIN + jnp.arange(per_part, dtype=jnp.int32)

    def add_slot(slot_index, running):
        shift_now = lax.dynamic_index_in_dim(offsets, slot_index, 1, keepdims=False)
        window_index = own_clusters + shift_now
        source_geometry = jnp.take(local_geometry, window_index, axis=1)
        source_values = jnp.take(sources, window_index + first_local, axis=1)
        live_mask = (slot_index < live_counts).astype(jnp.float32)
        near_block = (
            kernel_entries(target_geometry, source_geometry) * live_mask[:, None, None]
        ).astype(jnp.bfloat16)
        return running + jnp.einsum(
            "rcs,cts->rct", source_values, near_block, preferred_element_type=jnp.float32
        )

    start_sum = jnp.zeros((all_rows, per_part, panels), jnp.float32)
    near_part = lax.fori_loop(0, NNEAR, add_slot, start_sum)
    near_field = lax.all_to_all(
        near_part.reshape(all_rows, per_part * panels).astype(jnp.bfloat16),
        "rhs",
        split_axis=0,
        concat_axis=1,
        tiled=True,
    ).astype(jnp.float32)
    own_values = potential.astype(jnp.bfloat16).reshape(rows_here, clusters, panels)
    coefficients = jnp.einsum(
        "rcp,cpk->rck", own_values, col_basis, preferred_element_type=jnp.float32
    ).astype(jnp.bfloat16)
    rim_coefs = with_halo(
        coefficients.reshape(rows_here, clusters * basis_rank), (("leaf", 1),), FWIN * basis_rank
    )
    rim_coefs = rim_coefs.reshape(rows_here, clusters + 2 * FWIN, basis_rank)
    partner_index = jnp.arange(clusters, dtype=jnp.int32)[:, None] + FWIN + far_offset
    partners = jnp.take(rim_coefs, partner_index.reshape(-1), axis=1).reshape(
        rows_here, clusters, partners_count, basis_rank
    )
    leaf_far = jnp.einsum(
        "rcmk,cmkj->rcj", partners, leaf_coupling, preferred_element_type=jnp.float32
    )
    device_coef = jnp.einsum(
        "rck,ckj->rj", coefficients, leaf_up, preferred_element_type=jnp.float32
    ).astype(jnp.bfloat16)
    levels = lax.axis_size("leaf").bit_length() - 1
    device_index = lax.axis_index("leaf")
    couplings = []
    side_bits = []
    current = device_coef
    for tree_level in range(levels):
        side_bit = device_index // 2**tree_level % 2
        sibling = from_partner(current, "leaf", tree_level)
        couplings.append(
            jnp.dot(
                sibling, select_side(sibling_coupling, side_bit), preferred_element_type=jnp.float32
            )
        )
        side_bits.append(side_bit)
        if tree_level + 1 < levels:
            upward = jnp.dot(
                current, select_side(up_transfer, side_bit), preferred_element_type=jnp.float32
            )
            upward = upward + jnp.dot(
                sibling, select_side(up_transfer, 1 - side_bit), preferred_element_type=jnp.float32
            )
            current = upward.astype(jnp.bfloat16)
    local_sum = jnp.zeros((rows_here, basis_rank), jnp.float32)
    for tree_level in reversed(range(levels)):
        step_down = select_side(down_transfer, side_bits[tree_level]).astype(jnp.float32)
        local_sum = couplings[tree_level] + jnp.dot(
            local_sum, step_down, precision=lax.Precision.HIGHEST
        )
    leaf_local = leaf_far + jnp.einsum(
        "rk,ckj->rcj", local_sum, leaf_down.astype(jnp.float32), precision=lax.Precision.HIGHEST
    )
    leaf_local = leaf_local.astype(jnp.bfloat16)
    far_field = jnp.einsum(
        "rck,cpk->rcp", leaf_local, row_basis, preferred_element_type=jnp.float32
    )
    return near_field + far_field.reshape(rows_here, clusters * panels)


def solution(mesh):
    placed = (
        P("rhs", "leaf"),
        P(None, "leaf"),
        P("leaf"),
        P("leaf", None),
        P("leaf", None),
        P("leaf", None, None),
        P("leaf", None, None),
        P("leaf", None, None),
        P("leaf", None, None),
        P("leaf", None, None, None),
        P(),
        P(),
        P(),
    )
    return jax.shard_map(
        per_device, mesh=mesh, in_specs=placed, out_specs=P("rhs", "leaf"), check_vma=False
    )
```

profile of v0, /device:TPU:1, one launch (start us, length us, event | category | flops | bytes accessed | tf_op | source)
XLA Modules:
  0.0 244.2 jit_solution(15858377557532260188)
XLA Ops:
  9.3 8.8 %collective-permute-start.4 = (bf16[32,64]{1,0:T(8,128)(2,1)S(1)}, bf16[32,64]{1,0:T(8,128)(2,1)S(1)}, u32[]{:S(2)}, u32[]{:S(2)}) collective-permute-start(bf16[32,64]{1,0:T(8,128)(2,1)S(1)} %fusion.23), channel_id=1, source_target_pairs={{0,4},{4,0},{8,12},{12,8},{16,20},{20,16},{24,28},{28,24},{32,36},... | collective-permute-start | bytes 12296 | tf_op jit(solution)/shard_map/ppermute | solution.py:26
  24.1 3.0 %collective-permute-start.3 = (bf16[32,512]{1,0:T(8,128)(2,1)}, bf16[32,512]{1,0:T(8,128)(2,1)}, u32[]{:S(2)}, u32[]{:S(2)}) collective-permute-start(bf16[32,512]{1,0:T(8,128)(2,1)} %get-tuple-element.251), channel_id=1, source_target_pairs={{4,0},{8,4},{12,8},{16,12},{20,16},{24,20},{28,24},{32,28},{36,32}... | collective-permute-start | bytes 98312 | tf_op jit(solution)/shard_map/ppermute | solution.py:20
  28.8 2.5 %collective-permute-start = (f32[36,1536]{1,0:T(8,128)}, f32[36,1536]{1,0:T(8,128)}, u32[]{:S(2)}, u32[]{:S(2)}) collective-permute-start(f32[36,1536]{1,0:T(8,128)} %get-tuple-element.246), channel_id=1, source_target_pairs={{0,4},{4,8},{8,12},{12,16},{16,20},{20,24},{24,28},{28,32},{32,36}... | collective-permute-start | bytes 663560 | tf_op jit(solution)/shard_map/ppermute | solution.py:19
  31.4 2.4 %collective-permute-start.1 = (f32[36,1536]{1,0:T(8,128)}, f32[36,1536]{1,0:T(8,128)}, u32[]{:S(2)}, u32[]{:S(2)}) collective-permute-start(f32[36,1536]{1,0:T(8,128)} %get-tuple-element.247), channel_id=1, source_target_pairs={{4,0},{8,4},{12,8},{16,12},{20,16},{24,20},{28,24},{32,28},{36,32}... | collective-permute-start | bytes 663560 | tf_op jit(solution)/shard_map/ppermute | solution.py:20
  38.3 2.7 %collective-permute-done.5 = bf16[32,64]{1,0:T(8,128)(2,1)S(1)} collective-permute-done((bf16[32,64]{1,0:T(8,128)(2,1)S(1)}, bf16[32,64]{1,0:T(8,128)(2,1)S(1)}, u32[]{:S(2)}, u32[]{:S(2)}) %collective-permute-start.5) | collective-permute-done | bytes 4128 | tf_op jit(solution)/shard_map/ppermute | solution.py:26
  43.2 3.2 %collective-permute-done.6 = bf16[32,64]{1,0:T(8,128)(2,1)S(1)} collective-permute-done((bf16[32,64]{1,0:T(8,128)(2,1)S(1)}, bf16[32,64]{1,0:T(8,128)(2,1)S(1)}, u32[]{:S(2)}, u32[]{:S(2)}) %collective-permute-start.6) | collective-permute-done | bytes 4128 | tf_op jit(solution)/shard_map/ppermute | solution.py:26
  46.6 2.4 collective-permute-start.7
  49.1 5.7 %collective-permute-done.7 = bf16[32,64]{1,0:T(8,128)(2,1)S(1)} collective-permute-done((bf16[32,64]{1,0:T(8,128)(2,1)S(1)}, bf16[32,64]{1,0:T(8,128)(2,1)S(1)}, u32[]{:S(2)}, u32[]{:S(2)}) %collective-permute-start.7) | collective-permute-done | bytes 4128 | tf_op jit(solution)/shard_map/ppermute | solution.py:26
  58.4 2.4 pad_maximum_fusion
  64.1 5.0 %collective-permute-start.9 = (bf16[32,64]{1,0:T(8,128)(2,1)S(1)}, bf16[32,64]{1,0:T(8,128)(2,1)S(1)}, u32[]{:S(2)}, u32[]{:S(2)}) collective-permute-start(bf16[32,64]{1,0:T(8,128)(2,1)S(1)} %fusion.28), channel_id=1, source_target_pairs={{0,128},{4,132},{8,136},{12,140},{16,144},{20,148},{24,152},{28,15... | collective-permute-start | bytes 12296 | tf_op jit(solution)/shard_map/ppermute | solution.py:26
  70.3 8.3 %collective-permute-start.10 = (bf16[32,64]{1,0:T(8,128)(2,1)S(1)}, bf16[32,64]{1,0:T(8,128)(2,1)S(1)}, u32[]{:S(2)}, u32[]{:S(2)}) collective-permute-start(bf16[32,64]{1,0:T(8,128)(2,1)S(1)} %fusion.29), channel_id=1, source_target_pairs={{0,256},{4,260},{8,264},{12,268},{16,272},{20,276},{24,280},{28,28... | collective-permute-start | bytes 12296 | tf_op jit(solution)/shard_map/ppermute | solution.py:26
  91.8 21.3 %all-gather.2.cloned.1.call-done = bf16[128,11264]{1,0:T(8,128)(2,1)} async-done(((bf16[32,11264]{1,0:T(8,128)(2,1)}), bf16[128,11264]{1,0:T(8,128)(2,1)}) %all-gather.2.cloned.1.call-update) | async-done | bytes 2883600 | tf_op jit(solution)/shard_map/all_gather | solution.py:69
  113.1 4.6 %copy.43 = bf16[128,11264]{0,1:T(8,128)(2,1)} copy(bf16[128,11264]{1,0:T(8,128)(2,1)} %all-gather.2.cloned.1.call-done) | data formatting | bytes 5767168 | tf_op jit(solution)/shard_map/all_gather | solution.py:69
  117.6 4.6 %copy.45 = bf16[128,44,256]{2,0,1:T(8,128)(2,1)} copy(bf16[128,44,256]{0,2,1:T(8,128)(2,1)} %bitcast.197) | data formatting | bytes 5767168
  122.2 96.9 %while.14 = (s32[]{:T(128)}, f32[128,8,256]{0,2,1:T(8,128)}, s32[8,12]{0,1:T(8,128)}, f32[4,20,256]{2,0,1:T(4,128)S(1)}, f32[4,8,256]{2,1,0:T(8,128)S(1)}, /*ind...) while((s32[]{:T(128)}, f32[128,8,256]{0,2,1:T(8,128)}, ...), condition=%wide.region_1.2_spmd.clone, body=%wide.region_0.1_spmd.clone.sunk | while | flops 142354592 | bytes 4071995 | solution.py:93
  123.6 2.4 gather_fusion.1
  126.1 2.9 %fusion.174 = f32[128,8,256]{0,2,1:T(8,128)} fusion(f32[128,8,256]{0,2,1:T(8,128)} %get-tuple-element.342, f32[8]{0:T(128)S(1)} %compare_convert_fusion.2, f32[8,256]{1,0:T(8,128)S(1)} %get-tuple-element.316, f32[8,256]{1,0:T(8,128)S(1)} %get-tuple-element.320, f32[8,256]{1,0:T(8,128)S(1)} %get-tuple-element.321, ...), kind=kOutput, calls=%fused_computation.6.clone.1 | convolution fusion | flops 142344192 | bytes 2687017 | tf_op jit(solution)/shard_map/while/body/eval_jaxpr/rcs,cts->rct/dot_general | solution.py:88
  130.5 2.4 gather_fusion.1
  132.9 4.3 %fusion.174 = f32[128,8,256]{0,2,1:T(8,128)} fusion(f32[128,8,256]{0,2,1:T(8,128)} %get-tuple-element.342, f32[8]{0:T(128)S(1)} %compare_convert_fusion.2, f32[8,256]{1,0:T(8,128)S(1)} %get-tuple-element.316, f32[8,256]{1,0:T(8,128)S(1)} %get-tuple-element.320, f32[8,256]{1,0:T(8,128)S(1)} %get-tuple-element.321, ...), kind=kOutput, calls=%fused_computation.6.clone.1 | convolution fusion | flops 142344192 | bytes 2687017 | tf_op jit(solution)/shard_map/while/body/eval_jaxpr/rcs,cts->rct/dot_general | solution.py:88
  138.6 2.4 gather_fusion.1
  141.1 4.3 %fusion.174 = f32[128,8,256]{0,2,1:T(8,128)} fusion(f32[128,8,256]{0,2,1:T(8,128)} %get-tuple-element.342, f32[8]{0:T(128)S(1)} %compare_convert_fusion.2, f32[8,256]{1,0:T(8,128)S(1)} %get-tuple-element.316, f32[8,256]{1,0:T(8,128)S(1)} %get-tuple-element.320, f32[8,256]{1,0:T(8,128)S(1)} %get-tuple-element.321, ...), kind=kOutput, calls=%fused_computation.6.clone.1 | convolution fusion | flops 142344192 | bytes 2687017 | tf_op jit(solution)/shard_map/while/body/eval_jaxpr/rcs,cts->rct/dot_general | solution.py:88
  149.3 4.3 %fusion.174 = f32[128,8,256]{0,2,1:T(8,128)} fusion(f32[128,8,256]{0,2,1:T(8,128)} %get-tuple-element.342, f32[8]{0:T(128)S(1)} %compare_convert_fusion.2, f32[8,256]{1,0:T(8,128)S(1)} %get-tuple-element.316, f32[8,256]{1,0:T(8,128)S(1)} %get-tuple-element.320, f32[8,256]{1,0:T(8,128)S(1)} %get-tuple-element.321, ...), kind=kOutput, calls=%fused_computation.6.clone.1 | convolution fusion | flops 142344192 | bytes 2687017 | tf_op jit(solution)/shard_map/while/body/eval_jaxpr/rcs,cts->rct/dot_general | solution.py:88
  157.4 4.3 %fusion.174 = f32[128,8,256]{0,2,1:T(8,128)} fusion(f32[128,8,256]{0,2,1:T(8,128)} %get-tuple-element.342, f32[8]{0:T(128)S(1)} %compare_convert_fusion.2, f32[8,256]{1,0:T(8,128)S(1)} %get-tuple-element.316, f32[8,256]{1,0:T(8,128)S(1)} %get-tuple-element.320, f32[8,256]{1,0:T(8,128)S(1)} %get-tuple-element.321, ...), kind=kOutput, calls=%fused_computation.6.clone.1 | convolution fusion | flops 142344192 | bytes 2687017 | tf_op jit(solution)/shard_map/while/body/eval_jaxpr/rcs,cts->rct/dot_general | solution.py:88
  165.6 4.3 %fusion.174 = f32[128,8,256]{0,2,1:T(8,128)} fusion(f32[128,8,256]{0,2,1:T(8,128)} %get-tuple-element.342, f32[8]{0:T(128)S(1)} %compare_convert_fusion.2, f32[8,256]{1,0:T(8,128)S(1)} %get-tuple-element.316, f32[8,256]{1,0:T(8,128)S(1)} %get-tuple-element.320, f32[8,256]{1,0:T(8,128)S(1)} %get-tuple-element.321, ...), kind=kOutput, calls=%fused_computation.6.clone.1 | convolution fusion | flops 142344192 | bytes 2687017 | tf_op jit(solution)/shard_map/while/body/eval_jaxpr/rcs,cts->rct/dot_general | solution.py:88
  173.8 4.3 %fusion.174 = f32[128,8,256]{0,2,1:T(8,128)} fusion(f32[128,8,256]{0,2,1:T(8,128)} %get-tuple-element.342, f32[8]{0:T(128)S(1)} %compare_convert_fusion.2, f32[8,256]{1,0:T(8,128)S(1)} %get-tuple-element.316, f32[8,256]{1,0:T(8,128)S(1)} %get-tuple-element.320, f32[8,256]{1,0:T(8,128)S(1)} %get-tuple-element.321, ...), kind=kOutput, calls=%fused_computation.6.clone.1 | convolution fusion | flops 142344192 | bytes 2687017 | tf_op jit(solution)/shard_map/while/body/eval_jaxpr/rcs,cts->rct/dot_general | solution.py:88
  182.0 4.3 %fusion.174 = f32[128,8,256]{0,2,1:T(8,128)} fusion(f32[128,8,256]{0,2,1:T(8,128)} %get-tuple-element.342, f32[8]{0:T(128)S(1)} %compare_convert_fusion.2, f32[8,256]{1,0:T(8,128)S(1)} %get-tuple-element.316, f32[8,256]{1,0:T(8,128)S(1)} %get-tuple-element.320, f32[8,256]{1,0:T(8,128)S(1)} %get-tuple-element.321, ...), kind=kOutput, calls=%fused_computation.6.clone.1 | convolution fusion | flops 142344192 | bytes 2687017 | tf_op jit(solution)/shard_map/while/body/eval_jaxpr/rcs,cts->rct/dot_general | solution.py:88
  190.2 4.3 %fusion.174 = f32[128,8,256]{0,2,1:T(8,128)} fusion(f32[128,8,256]{0,2,1:T(8,128)} %get-tuple-element.342, f32[8]{0:T(128)S(1)} %compare_convert_fusion.2, f32[8,256]{1,0:T(8,128)S(1)} %get-tuple-element.316, f32[8,256]{1,0:T(8,128)S(1)} %get-tuple-element.320, f32[8,256]{1,0:T(8,128)S(1)} %get-tuple-element.321, ...), kind=kOutput, calls=%fused_computation.6.clone.1 | convolution fusion | flops 142344192 | bytes 2687017 | tf_op jit(solution)/shard_map/while/body/eval_jaxpr/rcs,cts->rct/dot_general | solution.py:88
  198.4 4.3 %fusion.174 = f32[128,8,256]{0,2,1:T(8,128)} fusion(f32[128,8,256]{0,2,1:T(8,128)} %get-tuple-element.342, f32[8]{0:T(128)S(1)} %compare_convert_fusion.2, f32[8,256]{1,0:T(8,128)S(1)} %get-tuple-element.316, f32[8,256]{1,0:T(8,128)S(1)} %get-tuple-element.320, f32[8,256]{1,0:T(8,128)S(1)} %get-tuple-element.321, ...), kind=kOutput, calls=%fused_computation.6.clone.1 | convolution fusion | flops 142344192 | bytes 2687017 | tf_op jit(solution)/shard_map/while/body/eval_jaxpr/rcs,cts->rct/dot_general | solution.py:88
  206.6 4.3 %fusion.174 = f32[128,8,256]{0,2,1:T(8,128)} fusion(f32[128,8,256]{0,2,1:T(8,128)} %get-tuple-element.342, f32[8]{0:T(128)S(1)} %compare_convert_fusion.2, f32[8,256]{1,0:T(8,128)S(1)} %get-tuple-element.316, f32[8,256]{1,0:T(8,128)S(1)} %get-tuple-element.320, f32[8,256]{1,0:T(8,128)S(1)} %get-tuple-element.321, ...), kind=kOutput, calls=%fused_computation.6.clone.1 | convolution fusion | flops 142344192 | bytes 2687017 | tf_op jit(solution)/shard_map/while/body/eval_jaxpr/rcs,cts->rct/dot_general | solution.py:88
  214.8 4.3 %fusion.174 = f32[128,8,256]{0,2,1:T(8,128)} fusion(f32[128,8,256]{0,2,1:T(8,128)} %get-tuple-element.342, f32[8]{0:T(128)S(1)} %compare_convert_fusion.2, f32[8,256]{1,0:T(8,128)S(1)} %get-tuple-element.316, f32[8,256]{1,0:T(8,128)S(1)} %get-tuple-element.320, f32[8,256]{1,0:T(8,128)S(1)} %get-tuple-element.321, ...), kind=kOutput, calls=%fused_computation.6.clone.1 | convolution fusion | flops 142344192 | bytes 2687017 | tf_op jit(solution)/shard_map/while/body/eval_jaxpr/rcs,cts->rct/dot_general | solution.py:88
  221.9 4.1 %all-to-all-start = ((bf16[4,32,2048]{2,1,0:T(8,128)(2,1)}), bf16[4,32,2048]{2,1,0:T(8,128)(2,1)}, u32[]{:S(2)}, u32[]{:S(2)}) async-start(bf16[4,32,2048]{2,1,0:T(8,128)(2,1)} %convert_element_type.77), calls=%async_computation | async-start | bytes 1048576 | tf_op jit(solution)/shard_map/all_to_all | solution.py:94
  229.1 6.0 %all-to-all-done = bf16[4,32,2048]{2,1,0:T(8,128)(2,1)} async-done(((bf16[4,32,2048]{2,1,0:T(8,128)(2,1)}), bf16[4,32,2048]{2,1,0:T(8,128)(2,1)}, u32[]{:S(2)}, u32[]{:S(2)}) %all-to-all-start) | async-done | bytes 524320 | tf_op jit(solution)/shard_map/all_to_all | solution.py:94
  (261 shorter events, 84.7 us)
Async XLA Ops:
  6.5 80.3 %copy-start = (bf16[32,4,64,64]{3,2,1,0:T(8,128)(2,1)S(1)}, bf16[32,4,64,64]{3,2,1,0:T(8,128)(2,1)}, u32[]{:S(2)}) copy-start(bf16[32,4,64,64]{3,2,1,0:T(8,128)(2,1)} %param.24) | copy-start | bytes 3145732
  6.5 106.5 %all-gather.2.cloned.1.call-start = ((), (), s32[]{:S(2)}) async-start(), calls=%async_computation.1 | async-start | bytes 3604480 | tf_op jit(solution)/shard_map/all_gather | solution.py:69
  6.5 2.0 copy-start.3
  6.5 2.4 copy-start.5
  9.0 25.0 %copy-start.13 = (s32[32,4]{0,1:T(4,128)S(1)}, s32[32,4]{0,1:T(4,128)}, u32[]{:S(2)}) copy-start(s32[32,4]{0,1:T(4,128)} %param.19) | copy-start | bytes 1540
  9.0 26.3 %copy-start.2 = (bf16[2,64,64]{2,1,0:T(8,128)(2,1)S(1)}, bf16[2,64,64]{2,1,0:T(8,128)(2,1)}, u32[]{:S(2)}) copy-start(bf16[2,64,64]{2,1,0:T(8,128)(2,1)} %param.25) | copy-start | bytes 49156
  9.0 26.4 %copy-start.6 = (bf16[2,64,64]{2,1,0:T(8,128)(2,1)S(1)}, bf16[2,64,64]{2,1,0:T(8,128)(2,1)}, u32[]{:S(2)}) copy-start(bf16[2,64,64]{2,1,0:T(8,128)(2,1)} %param.26) | copy-start | bytes 49156
  9.0 26.5 %copy-start.12 = (s32[32,12]{0,1:T(8,128)S(1)}, s32[32,12]{0,1:T(8,128)}, u32[]{:S(2)}) copy-start(s32[32,12]{0,1:T(8,128)} %param.18) | copy-start | bytes 4612
  9.3 26.9 %collective-permute-start.4 = (bf16[32,64]{1,0:T(8,128)(2,1)S(1)}, bf16[32,64]{1,0:T(8,128)(2,1)S(1)}, u32[]{:S(2)}, u32[]{:S(2)}) collective-permute-start(bf16[32,64]{1,0:T(8,128)(2,1)S(1)} %fusion.23), channel_id=1, source_target_pairs={{0,4},{4,0},{8,12},{12,8},{16,20},{20,16},{24,28},{28,24},{32,36},... | collective-permute-start | bytes 12296 | tf_op jit(solution)/shard_map/ppermute | solution.py:26
  22.2 62.5 %collective-permute-start.2 = (bf16[32,512]{1,0:T(8,128)(2,1)}, bf16[32,512]{1,0:T(8,128)(2,1)}, u32[]{:S(2)}, u32[]{:S(2)}) collective-permute-start(bf16[32,512]{1,0:T(8,128)(2,1)} %get-tuple-element.250), channel_id=1, source_target_pairs={{0,4},{4,8},{8,12},{12,16},{16,20},{20,24},{24,28},{28,32},{32,36}... | collective-permute-start | bytes 98312 | tf_op jit(solution)/shard_map/ppermute | solution.py:19
  24.1 60.6 %collective-permute-start.3 = (bf16[32,512]{1,0:T(8,128)(2,1)}, bf16[32,512]{1,0:T(8,128)(2,1)}, u32[]{:S(2)}, u32[]{:S(2)}) collective-permute-start(bf16[32,512]{1,0:T(8,128)(2,1)} %get-tuple-element.251), channel_id=1, source_target_pairs={{4,0},{8,4},{12,8},{16,12},{20,16},{24,20},{28,24},{32,28},{36,32}... | collective-permute-start | bytes 98312 | tf_op jit(solution)/shard_map/ppermute | solution.py:20
  28.8 29.5 %collective-permute-start = (f32[36,1536]{1,0:T(8,128)}, f32[36,1536]{1,0:T(8,128)}, u32[]{:S(2)}, u32[]{:S(2)}) collective-permute-start(f32[36,1536]{1,0:T(8,128)} %get-tuple-element.246), channel_id=1, source_target_pairs={{0,4},{4,8},{8,12},{12,16},{16,20},{20,24},{24,28},{28,32},{32,36}... | collective-permute-start | bytes 663560 | tf_op jit(solution)/shard_map/ppermute | solution.py:19
  31.4 27.0 %collective-permute-start.1 = (f32[36,1536]{1,0:T(8,128)}, f32[36,1536]{1,0:T(8,128)}, u32[]{:S(2)}, u32[]{:S(2)}) collective-permute-start(f32[36,1536]{1,0:T(8,128)} %get-tuple-element.247), channel_id=1, source_target_pairs={{4,0},{8,4},{12,8},{16,12},{20,16},{24,20},{28,24},{32,28},{36,32}... | collective-permute-start | bytes 663560 | tf_op jit(solution)/shard_map/ppermute | solution.py:20
  36.2 21.3 %copy-start.8 = (bf16[32,64]{1,0:T(8,128)(2,1)}, bf16[32,64]{1,0:T(8,128)(2,1)S(1)}, u32[]{:S(2)}) copy-start(bf16[32,64]{1,0:T(8,128)(2,1)S(1)} %collective-permute-done.4) | copy-start | bytes 12292
  36.3 4.7 %collective-permute-start.5 = (bf16[32,64]{1,0:T(8,128)(2,1)S(1)}, bf16[32,64]{1,0:T(8,128)(2,1)S(1)}, u32[]{:S(2)}, u32[]{:S(2)}) collective-permute-start(bf16[32,64]{1,0:T(8,128)(2,1)S(1)} %fusion.24), channel_id=1, source_target_pairs={{0,8},{4,12},{8,0},{12,4},{16,24},{20,28},{24,16},{28,20},{32,40},... | collective-permute-start | bytes 12296 | tf_op jit(solution)/shard_map/ppermute | solution.py:26
  41.1 5.3 %collective-permute-start.6 = (bf16[32,64]{1,0:T(8,128)(2,1)S(1)}, bf16[32,64]{1,0:T(8,128)(2,1)S(1)}, u32[]{:S(2)}, u32[]{:S(2)}) collective-permute-start(bf16[32,64]{1,0:T(8,128)(2,1)S(1)} %fusion.25), channel_id=1, source_target_pairs={{0,16},{4,20},{8,24},{12,28},{16,0},{20,4},{24,8},{28,12},{32,48},... | collective-permute-start | bytes 12296 | tf_op jit(solution)/shard_map/ppermute | solution.py:26
  46.6 8.3 %collective-permute-start.7 = (bf16[32,64]{1,0:T(8,128)(2,1)S(1)}, bf16[32,64]{1,0:T(8,128)(2,1)S(1)}, u32[]{:S(2)}, u32[]{:S(2)}) collective-permute-start(bf16[32,64]{1,0:T(8,128)(2,1)S(1)} %fusion.26), channel_id=1, source_target_pairs={{0,32},{4,36},{8,40},{12,44},{16,48},{20,52},{24,56},{28,60},{32,0... | collective-permute-start | bytes 12296 | tf_op jit(solution)/shard_map/ppermute | solution.py:26
  54.9 2.7 %copy-start.10 = (bf16[32,64]{1,0:T(8,128)(2,1)}, bf16[32,64]{1,0:T(8,128)(2,1)S(1)}, u32[]{:S(2)}) copy-start(bf16[32,64]{1,0:T(8,128)(2,1)S(1)} %collective-permute-done.7) | copy-start | bytes 12292
  55.6 7.6 %collective-permute-start.8 = (bf16[32,64]{1,0:T(8,128)(2,1)}, bf16[32,64]{1,0:T(8,128)(2,1)}, u32[]{:S(2)}, u32[]{:S(2)}) collective-permute-start(bf16[32,64]{1,0:T(8,128)(2,1)} %fusion.27), channel_id=1, source_target_pairs={{0,64},{4,68},{8,72},{12,76},{16,80},{20,84},{24,88},{28,92},{32,9... | collective-permute-start | bytes 12296 | tf_op jit(solution)/shard_map/ppermute | solution.py:26
  58.4 23.8 %copy-start.7 = (bf16[2,64,64]{2,1,0:T(8,128)(2,1)S(1)}, bf16[2,64,64]{2,1,0:T(8,128)(2,1)}, u32[]{:S(2)}) copy-start(bf16[2,64,64]{2,1,0:T(8,128)(2,1)} %param.27) | copy-start | bytes 49156
  60.8 22.9 %copy-start.11 = (bf16[32,64]{1,0:T(8,128)(2,1)S(1)}, bf16[32,64]{1,0:T(8,128)(2,1)}, u32[]{:S(2)}) copy-start(bf16[32,64]{1,0:T(8,128)(2,1)} %copy-done.10) | copy-start | bytes 12292
  60.8 23.7 %copy-start.9 = (bf16[32,64]{1,0:T(8,128)(2,1)S(1)}, bf16[32,64]{1,0:T(8,128)(2,1)}, u32[]{:S(2)}) copy-start(bf16[32,64]{1,0:T(8,128)(2,1)} %copy-done.8) | copy-start | bytes 12292
  60.8 23.9 %copy-start.4 = (bf16[32,2048]{1,0:T(8,128)(2,1)S(1)}, bf16[32,2048]{1,0:T(8,128)(2,1)}, u32[]{:S(2)}) copy-start(bf16[32,2048]{1,0:T(8,128)(2,1)} %reshape.114) | copy-start | bytes 393220
  64.1 6.1 %collective-permute-start.9 = (bf16[32,64]{1,0:T(8,128)(2,1)S(1)}, bf16[32,64]{1,0:T(8,128)(2,1)S(1)}, u32[]{:S(2)}, u32[]{:S(2)}) collective-permute-start(bf16[32,64]{1,0:T(8,128)(2,1)S(1)} %fusion.28), channel_id=1, source_target_pairs={{0,128},{4,132},{8,136},{12,140},{16,144},{20,148},{24,152},{28,15... | collective-permute-start | bytes 12296 | tf_op jit(solution)/shard_map/ppermute | solution.py:26
  70.3 11.9 %collective-permute-start.10 = (bf16[32,64]{1,0:T(8,128)(2,1)S(1)}, bf16[32,64]{1,0:T(8,128)(2,1)S(1)}, u32[]{:S(2)}, u32[]{:S(2)}) collective-permute-start(bf16[32,64]{1,0:T(8,128)(2,1)S(1)} %fusion.29), channel_id=1, source_target_pairs={{0,256},{4,260},{8,264},{12,268},{16,272},{20,276},{24,280},{28,28... | collective-permute-start | bytes 12296 | tf_op jit(solution)/shard_map/ppermute | solution.py:26
  117.6 4.6 %copy-start.14 = (s32[8]{0:T(128)S(1)}, s32[8]{0:T(128)}, u32[]{:S(2)}) copy-start(s32[8]{0:T(128)} %dynamic_slice.98) | copy-start | bytes 100
  220.8 5.2 %copy-start.1 = (f32[32,32,64]{2,0,1:T(8,128)S(1)}, f32[32,32,64]{2,0,1:T(8,128)}, u32[]{:S(2)}) copy-start(f32[32,32,64]{2,0,1:T(8,128)} %convolution_bitcast_fusion.2) | copy-start | bytes 786436
  221.9 13.2 %all-to-all-start = ((bf16[4,32,2048]{2,1,0:T(8,128)(2,1)}), bf16[4,32,2048]{2,1,0:T(8,128)(2,1)}, u32[]{:S(2)}, u32[]{:S(2)}) async-start(bf16[4,32,2048]{2,1,0:T(8,128)(2,1)} %convert_element_type.77), calls=%async_computation | async-start | bytes 1048576 | tf_op jit(solution)/shard_map/all_to_all | solution.py:94
Sparse Core Ops, SparseCore 0:
  63.3 49.6 all-gather.1
where the time goes:
time: 247 us; the launch traced here: 244 us
  local copies, waits for them, and re-layouts  62.7 us (25%)
  matrix products  62.2 us (25%)
  starting transfers between devices  44.3 us (18%)
  waiting for transfers between devices  39.9 us (16%)
  other arithmetic  20.4 us (8%)
  between operations  13.9 us (6%)
    dot_general x12, matrix products, add_slot(): jnp.einsum('rcs,cts->rct', source_values, near_block, preferred_element_t...  50.4 us
    ppermute x7, starting transfers between devices, from_partner(): lax.ppermute(value, axis, [(i, i ^ 1 << apart) for i in range(lax.axis_si...  30.3 us
    gather x12, local copies, waits for them, and re-layouts, add_slot(): source_values = jnp.take(sources, window_index + first_local, axis=1)  28.7 us
    all_gather x1, waiting for transfers between devices, per_device(): sources = lax.all_gather(value_rows, 'rhs', axis=0, tiled=True)  21.3 us
    ppermute x7, waiting for transfers between devices, from_partner(): lax.ppermute(value, axis, [(i, i ^ 1 << apart) for i in range(lax.axis_si...  12.5 us
    reduce_and x12, other arithmetic, add_slot(): source_values = jnp.take(sources, window_index + first_local, axis=1)  8.28 us
    gather x12, local copies, waits for them, and re-layouts, add_slot(): source_geometry = jnp.take(local_geometry, window_index, axis=1)  6.92 us
    all_to_all x1, waiting for transfers between devices, per_device(): lax.all_to_all(near_part.reshape(all_rows, per_part * panels).astype(jnp....  6.04 us
  transfers between devices with their start and end apart: 13, of which 6 were waited for; matrix products, arithmetic and copies ran while one was open for 13% of the time, Pallas kernels for 0%

commit v1 on v0

--- a/solution.py
+++ b/solution.py
@@ -7,6 +7,13 @@
 NNEAR = 12
 NWIN = 6
 FWIN = 8
+
+
+def trade_parts(block, mesh_axis, split, join):
+    size = lax.axis_size(mesh_axis)
+    pieces = jnp.stack(jnp.split(block, size, axis=split), axis=0)
+    pieces = lax.all_to_all(pieces, mesh_axis, split_axis=0, concat_axis=0)
+    return jnp.concatenate(pieces, axis=join)
 
 
 def with_halo(value, sides, width):
@@ -91,12 +98,8 @@
 
     start_sum = jnp.zeros((all_rows, per_part, panels), jnp.float32)
     near_part = lax.fori_loop(0, NNEAR, add_slot, start_sum)
-    near_field = lax.all_to_all(
-        near_part.reshape(all_rows, per_part * panels).astype(jnp.bfloat16),
-        "rhs",
-        split_axis=0,
-        concat_axis=1,
-        tiled=True,
+    near_field = trade_parts(
+        near_part.reshape(all_rows, per_part * panels).astype(jnp.bfloat16), "rhs", 0, 1
     ).astype(jnp.float32)
     own_values = potential.astype(jnp.bfloat16).reshape(rows_here, clusters, panels)
     coefficients = jnp.einsum(

time: 247 us -> 252 us (1.020)
  local copies, waits for them, and re-layouts: 62.7 us -> 66.3 us
    another operation x0 -> x4, local copies, waits for them, and re-layouts: none -> 3.51 us  [trade_parts(): pieces = jnp.stack(jnp.split(block, size, axis=split), axis=0)]
where the time goes in v1:
time: 252 us; the launch traced here: 249 us
  local copies, waits for them, and re-layouts  66.3 us (26%)
  matrix products  61.2 us (24%)
  starting transfers between devices  44.4 us (18%)
  waiting for transfers between devices  40.4 us (16%)
  other arithmetic  22.2 us (9%)
  between operations  13.9 us (6%)
    dot_general x12, matrix products, add_slot(): jnp.einsum('rcs,cts->rct', source_values, near_block, preferred_element_t...  50.4 us
    ppermute x7, starting transfers between devices, from_partner(): lax.ppermute(value, axis, [(i, i ^ 1 << apart) for i in range(lax.axis_si...  30.4 us
    gather x12, local copies, waits for them, and re-layouts, add_slot(): source_values = jnp.take(sources, window_index + first_local, axis=1)  28.7 us
    all_gather x1, waiting for transfers between devices, per_device(): sources = lax.all_gather(value_rows, 'rhs', axis=0, tiled=True)  20.9 us
    ppermute x7, waiting for transfers between devices, from_partner(): lax.ppermute(value, axis, [(i, i ^ 1 << apart) for i in range(lax.axis_si...  12.5 us
    reduce_and x12, other arithmetic, add_slot(): source_values = jnp.take(sources, window_index + first_local, axis=1)  8.26 us
    all_to_all x1, waiting for transfers between devices, trade_parts(): pieces = lax.all_to_all(pieces, mesh_axis, split_axis=0, concat_axis=0)  6.94 us
    gather x12, local copies, waits for them, and re-layouts, add_slot(): source_geometry = jnp.take(local_geometry, window_index, axis=1)  6.92 us
  transfers between devices with their start and end apart: 13, of which 6 were waited for; matrix products, arithmetic and copies ran while one was open for 13% of the time, Pallas kernels for 0%

profile of v1, /device:TPU:1, one launch (start us, length us, event | category | flops | bytes accessed | tf_op | source)
XLA Modules:
  0.0 249.3 jit_solution(5405785858266732042)
XLA Ops:
  9.3 8.8 %collective-permute-start.4 = (bf16[32,64]{1,0:T(8,128)(2,1)S(1)}, bf16[32,64]{1,0:T(8,128)(2,1)S(1)}, u32[]{:S(2)}, u32[]{:S(2)}) collective-permute-start(bf16[32,64]{1,0:T(8,128)(2,1)S(1)} %fusion.23), channel_id=1, source_target_pairs={{0,4},{4,0},{8,12},{12,8},{16,20},{20,16},{24,28},{28,24},{32,36},... | collective-permute-start | bytes 12296 | tf_op jit(solution)/shard_map/ppermute | solution.py:33
  24.1 3.0 %collective-permute-start.3 = (bf16[32,512]{1,0:T(8,128)(2,1)}, bf16[32,512]{1,0:T(8,128)(2,1)}, u32[]{:S(2)}, u32[]{:S(2)}) collective-permute-start(bf16[32,512]{1,0:T(8,128)(2,1)} %get-tuple-element.255), channel_id=1, source_target_pairs={{4,0},{8,4},{12,8},{16,12},{20,16},{24,20},{28,24},{32,28},{36,32}... | collective-permute-start | bytes 98312 | tf_op jit(solution)/shard_map/ppermute | solution.py:27
  28.8 2.6 %collective-permute-start = (f32[36,1536]{1,0:T(8,128)}, f32[36,1536]{1,0:T(8,128)}, u32[]{:S(2)}, u32[]{:S(2)}) collective-permute-start(f32[36,1536]{1,0:T(8,128)} %get-tuple-element.246), channel_id=1, source_target_pairs={{0,4},{4,8},{8,12},{12,16},{16,20},{20,24},{24,28},{28,32},{32,36}... | collective-permute-start | bytes 663560 | tf_op jit(solution)/shard_map/ppermute | solution.py:26
  31.4 2.4 collective-permute-start.1
  38.4 2.6 %collective-permute-done.5 = bf16[32,64]{1,0:T(8,128)(2,1)S(1)} collective-permute-done((bf16[32,64]{1,0:T(8,128)(2,1)S(1)}, bf16[32,64]{1,0:T(8,128)(2,1)S(1)}, u32[]{:S(2)}, u32[]{:S(2)}) %collective-permute-start.5) | collective-permute-done | bytes 4128 | tf_op jit(solution)/shard_map/ppermute | solution.py:33
  43.2 3.2 %collective-permute-done.6 = bf16[32,64]{1,0:T(8,128)(2,1)S(1)} collective-permute-done((bf16[32,64]{1,0:T(8,128)(2,1)S(1)}, bf16[32,64]{1,0:T(8,128)(2,1)S(1)}, u32[]{:S(2)}, u32[]{:S(2)}) %collective-permute-start.6) | collective-permute-done | bytes 4128 | tf_op jit(solution)/shard_map/ppermute | solution.py:33
  46.5 2.5 collective-permute-start.7
  49.1 5.7 %collective-permute-done.7 = bf16[32,64]{1,0:T(8,128)(2,1)S(1)} collective-permute-done((bf16[32,64]{1,0:T(8,128)(2,1)S(1)}, bf16[32,64]{1,0:T(8,128)(2,1)S(1)}, u32[]{:S(2)}, u32[]{:S(2)}) %collective-permute-start.7) | collective-permute-done | bytes 4128 | tf_op jit(solution)/shard_map/ppermute | solution.py:33
  58.4 2.4 pad_maximum_fusion
  64.0 5.1 %collective-permute-start.9 = (bf16[32,64]{1,0:T(8,128)(2,1)S(1)}, bf16[32,64]{1,0:T(8,128)(2,1)S(1)}, u32[]{:S(2)}, u32[]{:S(2)}) collective-permute-start(bf16[32,64]{1,0:T(8,128)(2,1)S(1)} %fusion.28), channel_id=1, source_target_pairs={{0,128},{4,132},{8,136},{12,140},{16,144},{20,148},{24,152},{28,15... | collective-permute-start | bytes 12296 | tf_op jit(solution)/shard_map/ppermute | solution.py:33
  70.3 8.3 %collective-permute-start.10 = (bf16[32,64]{1,0:T(8,128)(2,1)S(1)}, bf16[32,64]{1,0:T(8,128)(2,1)S(1)}, u32[]{:S(2)}, u32[]{:S(2)}) collective-permute-start(bf16[32,64]{1,0:T(8,128)(2,1)S(1)} %fusion.29), channel_id=1, source_target_pairs={{0,256},{4,260},{8,264},{12,268},{16,272},{20,276},{24,280},{28,28... | collective-permute-start | bytes 12296 | tf_op jit(solution)/shard_map/ppermute | solution.py:33
  92.0 20.9 %all-gather.2.cloned.1.call-done = bf16[128,11264]{1,0:T(8,128)(2,1)} async-done(((bf16[32,11264]{1,0:T(8,128)(2,1)}), bf16[128,11264]{1,0:T(8,128)(2,1)}) %all-gather.2.cloned.1.call-update) | async-done | bytes 2883600 | tf_op jit(solution)/shard_map/all_gather | solution.py:76
  112.9 4.5 %copy.51 = bf16[128,11264]{0,1:T(8,128)(2,1)} copy(bf16[128,11264]{1,0:T(8,128)(2,1)} %all-gather.2.cloned.1.call-done) | data formatting | bytes 5767168 | tf_op jit(solution)/shard_map/all_gather | solution.py:76
  117.4 4.6 %copy.53 = bf16[128,44,256]{2,0,1:T(8,128)(2,1)} copy(bf16[128,44,256]{0,2,1:T(8,128)(2,1)} %bitcast.201) | data formatting | bytes 5767168
  122.0 96.9 %while.14 = (s32[]{:T(128)}, f32[128,8,256]{0,2,1:T(8,128)}, s32[8,12]{0,1:T(8,128)}, f32[4,20,256]{2,0,1:T(4,128)S(1)}, f32[4,8,256]{2,1,0:T(8,128)S(1)}, /*ind...) while((s32[]{:T(128)}, f32[128,8,256]{0,2,1:T(8,128)}, ...), condition=%wide.region_1.2_spmd.clone, body=%wide.region_0.1_spmd.clone.sunk | while | flops 142354592 | bytes 4071995 | solution.py:100
  123.4 2.4 gather_fusion.1
  125.9 2.9 %fusion.175 = f32[128,8,256]{0,2,1:T(8,128)} fusion(f32[128,8,256]{0,2,1:T(8,128)} %get-tuple-element.346, f32[8]{0:T(128)S(1)} %compare_convert_fusion.2, f32[8,256]{1,0:T(8,128)S(1)} %get-tuple-element.320, f32[8,256]{1,0:T(8,128)S(1)} %get-tuple-element.324, f32[8,256]{1,0:T(8,128)S(1)} %get-tuple-element.325, ...), kind=kOutput, calls=%fused_computation.6.clone.1 | convolution fusion | flops 142344192 | bytes 2687017 | tf_op jit(solution)/shard_map/while/body/eval_jaxpr/rcs,cts->rct/dot_general | solution.py:95
  130.3 2.4 gather_fusion.1
  132.7 4.3 %fusion.175 = f32[128,8,256]{0,2,1:T(8,128)} fusion(f32[128,8,256]{0,2,1:T(8,128)} %get-tuple-element.346, f32[8]{0:T(128)S(1)} %compare_convert_fusion.2, f32[8,256]{1,0:T(8,128)S(1)} %get-tuple-element.320, f32[8,256]{1,0:T(8,128)S(1)} %get-tuple-element.324, f32[8,256]{1,0:T(8,128)S(1)} %get-tuple-element.325, ...), kind=kOutput, calls=%fused_computation.6.clone.1 | convolution fusion | flops 142344192 | bytes 2687017 | tf_op jit(solution)/shard_map/while/body/eval_jaxpr/rcs,cts->rct/dot_general | solution.py:95
  138.5 2.4 gather_fusion.1
  140.9 4.3 %fusion.175 = f32[128,8,256]{0,2,1:T(8,128)} fusion(f32[128,8,256]{0,2,1:T(8,128)} %get-tuple-element.346, f32[8]{0:T(128)S(1)} %compare_convert_fusion.2, f32[8,256]{1,0:T(8,128)S(1)} %get-tuple-element.320, f32[8,256]{1,0:T(8,128)S(1)} %get-tuple-element.324, f32[8,256]{1,0:T(8,128)S(1)} %get-tuple-element.325, ...), kind=kOutput, calls=%fused_computation.6.clone.1 | convolution fusion | flops 142344192 | bytes 2687017 | tf_op jit(solution)/shard_map/while/body/eval_jaxpr/rcs,cts->rct/dot_general | solution.py:95
  149.1 4.3 %fusion.175 = f32[128,8,256]{0,2,1:T(8,128)} fusion(f32[128,8,256]{0,2,1:T(8,128)} %get-tuple-element.346, f32[8]{0:T(128)S(1)} %compare_convert_fusion.2, f32[8,256]{1,0:T(8,128)S(1)} %get-tuple-element.320, f32[8,256]{1,0:T(8,128)S(1)} %get-tuple-element.324, f32[8,256]{1,0:T(8,128)S(1)} %get-tuple-element.325, ...), kind=kOutput, calls=%fused_computation.6.clone.1 | convolution fusion | flops 142344192 | bytes 2687017 | tf_op jit(solution)/shard_map/while/body/eval_jaxpr/rcs,cts->rct/dot_general | solution.py:95
  157.3 4.3 %fusion.175 = f32[128,8,256]{0,2,1:T(8,128)} fusion(f32[128,8,256]{0,2,1:T(8,128)} %get-tuple-element.346, f32[8]{0:T(128)S(1)} %compare_convert_fusion.2, f32[8,256]{1,0:T(8,128)S(1)} %get-tuple-element.320, f32[8,256]{1,0:T(8,128)S(1)} %get-tuple-element.324, f32[8,256]{1,0:T(8,128)S(1)} %get-tuple-element.325, ...), kind=kOutput, calls=%fused_computation.6.clone.1 | convolution fusion | flops 142344192 | bytes 2687017 | tf_op jit(solution)/shard_map/while/body/eval_jaxpr/rcs,cts->rct/dot_general | solution.py:95
  165.5 4.3 %fusion.175 = f32[128,8,256]{0,2,1:T(8,128)} fusion(f32[128,8,256]{0,2,1:T(8,128)} %get-tuple-element.346, f32[8]{0:T(128)S(1)} %compare_convert_fusion.2, f32[8,256]{1,0:T(8,128)S(1)} %get-tuple-element.320, f32[8,256]{1,0:T(8,128)S(1)} %get-tuple-element.324, f32[8,256]{1,0:T(8,128)S(1)} %get-tuple-element.325, ...), kind=kOutput, calls=%fused_computation.6.clone.1 | convolution fusion | flops 142344192 | bytes 2687017 | tf_op jit(solution)/shard_map/while/body/eval_jaxpr/rcs,cts->rct/dot_general | solution.py:95
  173.6 4.3 %fusion.175 = f32[128,8,256]{0,2,1:T(8,128)} fusion(f32[128,8,256]{0,2,1:T(8,128)} %get-tuple-element.346, f32[8]{0:T(128)S(1)} %compare_convert_fusion.2, f32[8,256]{1,0:T(8,128)S(1)} %get-tuple-element.320, f32[8,256]{1,0:T(8,128)S(1)} %get-tuple-element.324, f32[8,256]{1,0:T(8,128)S(1)} %get-tuple-element.325, ...), kind=kOutput, calls=%fused_computation.6.clone.1 | convolution fusion | flops 142344192 | bytes 2687017 | tf_op jit(solution)/shard_map/while/body/eval_jaxpr/rcs,cts->rct/dot_general | solution.py:95
  181.8 4.3 %fusion.175 = f32[128,8,256]{0,2,1:T(8,128)} fusion(f32[128,8,256]{0,2,1:T(8,128)} %get-tuple-element.346, f32[8]{0:T(128)S(1)} %compare_convert_fusion.2, f32[8,256]{1,0:T(8,128)S(1)} %get-tuple-element.320, f32[8,256]{1,0:T(8,128)S(1)} %get-tuple-element.324, f32[8,256]{1,0:T(8,128)S(1)} %get-tuple-element.325, ...), kind=kOutput, calls=%fused_computation.6.clone.1 | convolution fusion | flops 142344192 | bytes 2687017 | tf_op jit(solution)/shard_map/while/body/eval_jaxpr/rcs,cts->rct/dot_general | solution.py:95
  190.0 4.3 %fusion.175 = f32[128,8,256]{0,2,1:T(8,128)} fusion(f32[128,8,256]{0,2,1:T(8,128)} %get-tuple-element.346, f32[8]{0:T(128)S(1)} %compare_convert_fusion.2, f32[8,256]{1,0:T(8,128)S(1)} %get-tuple-element.320, f32[8,256]{1,0:T(8,128)S(1)} %get-tuple-element.324, f32[8,256]{1,0:T(8,128)S(1)} %get-tuple-element.325, ...), kind=kOutput, calls=%fused_computation.6.clone.1 | convolution fusion | flops 142344192 | bytes 2687017 | tf_op jit(solution)/shard_map/while/body/eval_jaxpr/rcs,cts->rct/dot_general | solution.py:95
  198.2 4.3 %fusion.175 = f32[128,8,256]{0,2,1:T(8,128)} fusion(f32[128,8,256]{0,2,1:T(8,128)} %get-tuple-element.346, f32[8]{0:T(128)S(1)} %compare_convert_fusion.2, f32[8,256]{1,0:T(8,128)S(1)} %get-tuple-element.320, f32[8,256]{1,0:T(8,128)S(1)} %get-tuple-element.324, f32[8,256]{1,0:T(8,128)S(1)} %get-tuple-element.325, ...), kind=kOutput, calls=%fused_computation.6.clone.1 | convolution fusion | flops 142344192 | bytes 2687017 | tf_op jit(solution)/shard_map/while/body/eval_jaxpr/rcs,cts->rct/dot_general | solution.py:95
  206.4 4.3 %fusion.175 = f32[128,8,256]{0,2,1:T(8,128)} fusion(f32[128,8,256]{0,2,1:T(8,128)} %get-tuple-element.346, f32[8]{0:T(128)S(1)} %compare_convert_fusion.2, f32[8,256]{1,0:T(8,128)S(1)} %get-tuple-element.320, f32[8,256]{1,0:T(8,128)S(1)} %get-tuple-element.324, f32[8,256]{1,0:T(8,128)S(1)} %get-tuple-element.325, ...), kind=kOutput, calls=%fused_computation.6.clone.1 | convolution fusion | flops 142344192 | bytes 2687017 | tf_op jit(solution)/shard_map/while/body/eval_jaxpr/rcs,cts->rct/dot_general | solution.py:95
  214.6 4.3 %fusion.175 = f32[128,8,256]{0,2,1:T(8,128)} fusion(f32[128,8,256]{0,2,1:T(8,128)} %get-tuple-element.346, f32[8]{0:T(128)S(1)} %compare_convert_fusion.2, f32[8,256]{1,0:T(8,128)S(1)} %get-tuple-element.320, f32[8,256]{1,0:T(8,128)S(1)} %get-tuple-element.324, f32[8,256]{1,0:T(8,128)S(1)} %get-tuple-element.325, ...), kind=kOutput, calls=%fused_computation.6.clone.1 | convolution fusion | flops 142344192 | bytes 2687017 | tf_op jit(solution)/shard_map/while/body/eval_jaxpr/rcs,cts->rct/dot_general | solution.py:95
  227.0 4.1 %all-to-all-start = ((bf16[4,32,2048]{2,1,0:T(8,128)(2,1)}), bf16[4,32,2048]{2,1,0:T(8,128)(2,1)}, u32[]{:S(2)}, u32[]{:S(2)}) async-start(bf16[4,32,2048]{2,1,0:T(8,128)(2,1)} %pad_maximum_fusion.1), calls=%async_computation | async-start | bytes 1048576 | tf_op jit(solution)/shard_map/all_to_all | solution.py:15
  233.2 6.9 %all-to-all-done = bf16[4,32,2048]{2,1,0:T(8,128)(2,1)} async-done(((bf16[4,32,2048]{2,1,0:T(8,128)(2,1)}), bf16[4,32,2048]{2,1,0:T(8,128)(2,1)}, u32[]{:S(2)}, u32[]{:S(2)}) %all-to-all-start) | async-done | bytes 524320 | tf_op jit(solution)/shard_map/all_to_all | solution.py:15
  (267 shorter events, 89.2 us)
Async XLA Ops:
  6.5 80.4 %copy-start = (bf16[32,4,64,64]{3,2,1,0:T(8,128)(2,1)S(1)}, bf16[32,4,64,64]{3,2,1,0:T(8,128)(2,1)}, u32[]{:S(2)}) copy-start(bf16[32,4,64,64]{3,2,1,0:T(8,128)(2,1)} %param.24) | copy-start | bytes 3145732
  6.5 106.4 %all-gather.2.cloned.1.call-start = ((), (), s32[]{:S(2)}) async-start(), calls=%async_computation.1 | async-start | bytes 3604480 | tf_op jit(solution)/shard_map/all_gather | solution.py:76
  6.5 2.0 copy-start.3
  6.5 2.4 copy-start.5
  9.0 25.0 %copy-start.14 = (s32[32,4]{0,1:T(4,128)S(1)}, s32[32,4]{0,1:T(4,128)}, u32[]{:S(2)}) copy-start(s32[32,4]{0,1:T(4,128)} %param.19) | copy-start | bytes 1540
  9.0 26.3 %copy-start.2 = (bf16[2,64,64]{2,1,0:T(8,128)(2,1)S(1)}, bf16[2,64,64]{2,1,0:T(8,128)(2,1)}, u32[]{:S(2)}) copy-start(bf16[2,64,64]{2,1,0:T(8,128)(2,1)} %param.25) | copy-start | bytes 49156
  9.0 26.4 %copy-start.7 = (bf16[2,64,64]{2,1,0:T(8,128)(2,1)S(1)}, bf16[2,64,64]{2,1,0:T(8,128)(2,1)}, u32[]{:S(2)}) copy-start(bf16[2,64,64]{2,1,0:T(8,128)(2,1)} %param.26) | copy-start | bytes 49156
  9.0 26.5 %copy-start.13 = (s32[32,12]{0,1:T(8,128)S(1)}, s32[32,12]{0,1:T(8,128)}, u32[]{:S(2)}) copy-start(s32[32,12]{0,1:T(8,128)} %param.18) | copy-start | bytes 4612
  9.3 26.9 %collective-permute-start.4 = (bf16[32,64]{1,0:T(8,128)(2,1)S(1)}, bf16[32,64]{1,0:T(8,128)(2,1)S(1)}, u32[]{:S(2)}, u32[]{:S(2)}) collective-permute-start(bf16[32,64]{1,0:T(8,128)(2,1)S(1)} %fusion.23), channel_id=1, source_target_pairs={{0,4},{4,0},{8,12},{12,8},{16,20},{20,16},{24,28},{28,24},{32,36},... | collective-permute-start | bytes 12296 | tf_op jit(solution)/shard_map/ppermute | solution.py:33
  22.1 62.7 %collective-permute-start.2 = (bf16[32,512]{1,0:T(8,128)(2,1)}, bf16[32,512]{1,0:T(8,128)(2,1)}, u32[]{:S(2)}, u32[]{:S(2)}) collective-permute-start(bf16[32,512]{1,0:T(8,128)(2,1)} %get-tuple-element.254), channel_id=1, source_target_pairs={{0,4},{4,8},{8,12},{12,16},{16,20},{20,24},{24,28},{28,32},{32,36}... | collective-permute-start | bytes 98312 | tf_op jit(solution)/shard_map/ppermute | solution.py:26
  24.1 60.8 %collective-permute-start.3 = (bf16[32,512]{1,0:T(8,128)(2,1)}, bf16[32,512]{1,0:T(8,128)(2,1)}, u32[]{:S(2)}, u32[]{:S(2)}) collective-permute-start(bf16[32,512]{1,0:T(8,128)(2,1)} %get-tuple-element.255), channel_id=1, source_target_pairs={{4,0},{8,4},{12,8},{16,12},{20,16},{24,20},{28,24},{32,28},{36,32}... | collective-permute-start | bytes 98312 | tf_op jit(solution)/shard_map/ppermute | solution.py:27
  28.8 29.5 %collective-permute-start = (f32[36,1536]{1,0:T(8,128)}, f32[36,1536]{1,0:T(8,128)}, u32[]{:S(2)}, u32[]{:S(2)}) collective-permute-start(f32[36,1536]{1,0:T(8,128)} %get-tuple-element.246), channel_id=1, source_target_pairs={{0,4},{4,8},{8,12},{12,16},{16,20},{20,24},{24,28},{28,32},{32,36}... | collective-permute-start | bytes 663560 | tf_op jit(solution)/shard_map/ppermute | solution.py:26
  31.4 27.0 %collective-permute-start.1 = (f32[36,1536]{1,0:T(8,128)}, f32[36,1536]{1,0:T(8,128)}, u32[]{:S(2)}, u32[]{:S(2)}) collective-permute-start(f32[36,1536]{1,0:T(8,128)} %get-tuple-element.247), channel_id=1, source_target_pairs={{4,0},{8,4},{12,8},{16,12},{20,16},{24,20},{28,24},{32,28},{36,32}... | collective-permute-start | bytes 663560 | tf_op jit(solution)/shard_map/ppermute | solution.py:27
  36.2 21.3 %copy-start.9 = (bf16[32,64]{1,0:T(8,128)(2,1)}, bf16[32,64]{1,0:T(8,128)(2,1)S(1)}, u32[]{:S(2)}) copy-start(bf16[32,64]{1,0:T(8,128)(2,1)S(1)} %collective-permute-done.4) | copy-start | bytes 12292
  36.3 4.7 %collective-permute-start.5 = (bf16[32,64]{1,0:T(8,128)(2,1)S(1)}, bf16[32,64]{1,0:T(8,128)(2,1)S(1)}, u32[]{:S(2)}, u32[]{:S(2)}) collective-permute-start(bf16[32,64]{1,0:T(8,128)(2,1)S(1)} %fusion.24), channel_id=1, source_target_pairs={{0,8},{4,12},{8,0},{12,4},{16,24},{20,28},{24,16},{28,20},{32,40},... | collective-permute-start | bytes 12296 | tf_op jit(solution)/shard_map/ppermute | solution.py:33
  41.1 5.3 %collective-permute-start.6 = (bf16[32,64]{1,0:T(8,128)(2,1)S(1)}, bf16[32,64]{1,0:T(8,128)(2,1)S(1)}, u32[]{:S(2)}, u32[]{:S(2)}) collective-permute-start(bf16[32,64]{1,0:T(8,128)(2,1)S(1)} %fusion.25), channel_id=1, source_target_pairs={{0,16},{4,20},{8,24},{12,28},{16,0},{20,4},{24,8},{28,12},{32,48},... | collective-permute-start | bytes 12296 | tf_op jit(solution)/shard_map/ppermute | solution.py:33
  46.5 8.3 %collective-permute-start.7 = (bf16[32,64]{1,0:T(8,128)(2,1)S(1)}, bf16[32,64]{1,0:T(8,128)(2,1)S(1)}, u32[]{:S(2)}, u32[]{:S(2)}) collective-permute-start(bf16[32,64]{1,0:T(8,128)(2,1)S(1)} %fusion.26), channel_id=1, source_target_pairs={{0,32},{4,36},{8,40},{12,44},{16,48},{20,52},{24,56},{28,60},{32,0... | collective-permute-start | bytes 12296 | tf_op jit(solution)/shard_map/ppermute | solution.py:33
  54.8 2.7 %copy-start.11 = (bf16[32,64]{1,0:T(8,128)(2,1)}, bf16[32,64]{1,0:T(8,128)(2,1)S(1)}, u32[]{:S(2)}) copy-start(bf16[32,64]{1,0:T(8,128)(2,1)S(1)} %collective-permute-done.7) | copy-start | bytes 12292
  55.6 7.6 %collective-permute-start.8 = (bf16[32,64]{1,0:T(8,128)(2,1)}, bf16[32,64]{1,0:T(8,128)(2,1)}, u32[]{:S(2)}, u32[]{:S(2)}) collective-permute-start(bf16[32,64]{1,0:T(8,128)(2,1)} %fusion.27), channel_id=1, source_target_pairs={{0,64},{4,68},{8,72},{12,76},{16,80},{20,84},{24,88},{28,92},{32,9... | collective-permute-start | bytes 12296 | tf_op jit(solution)/shard_map/ppermute | solution.py:33
  58.3 24.0 %copy-start.8 = (bf16[2,64,64]{2,1,0:T(8,128)(2,1)S(1)}, bf16[2,64,64]{2,1,0:T(8,128)(2,1)}, u32[]{:S(2)}) copy-start(bf16[2,64,64]{2,1,0:T(8,128)(2,1)} %param.27) | copy-start | bytes 49156
  60.8 23.1 %copy-start.12 = (bf16[32,64]{1,0:T(8,128)(2,1)S(1)}, bf16[32,64]{1,0:T(8,128)(2,1)}, u32[]{:S(2)}) copy-start(bf16[32,64]{1,0:T(8,128)(2,1)} %copy-done.11) | copy-start | bytes 12292
  60.8 23.9 %copy-start.10 = (bf16[32,64]{1,0:T(8,128)(2,1)S(1)}, bf16[32,64]{1,0:T(8,128)(2,1)}, u32[]{:S(2)}) copy-start(bf16[32,64]{1,0:T(8,128)(2,1)} %copy-done.9) | copy-start | bytes 12292
  60.8 24.1 %copy-start.4 = (bf16[32,2048]{1,0:T(8,128)(2,1)S(1)}, bf16[32,2048]{1,0:T(8,128)(2,1)}, u32[]{:S(2)}) copy-start(bf16[32,2048]{1,0:T(8,128)(2,1)} %reshape.120) | copy-start | bytes 393220
  64.0 6.1 %collective-permute-start.9 = (bf16[32,64]{1,0:T(8,128)(2,1)S(1)}, bf16[32,64]{1,0:T(8,128)(2,1)S(1)}, u32[]{:S(2)}, u32[]{:S(2)}) collective-permute-start(bf16[32,64]{1,0:T(8,128)(2,1)S(1)} %fusion.28), channel_id=1, source_target_pairs={{0,128},{4,132},{8,136},{12,140},{16,144},{20,148},{24,152},{28,15... | collective-permute-start | bytes 12296 | tf_op jit(solution)/shard_map/ppermute | solution.py:33
  70.3 12.1 %collective-permute-start.10 = (bf16[32,64]{1,0:T(8,128)(2,1)S(1)}, bf16[32,64]{1,0:T(8,128)(2,1)S(1)}, u32[]{:S(2)}, u32[]{:S(2)}) collective-permute-start(bf16[32,64]{1,0:T(8,128)(2,1)S(1)} %fusion.29), channel_id=1, source_target_pairs={{0,256},{4,260},{8,264},{12,268},{16,272},{20,276},{24,280},{28,28... | collective-permute-start | bytes 12296 | tf_op jit(solution)/shard_map/ppermute | solution.py:33
  117.4 4.6 %copy-start.15 = (s32[8]{0:T(128)S(1)}, s32[8]{0:T(128)}, u32[]{:S(2)}) copy-start(s32[8]{0:T(128)} %dynamic_slice.98) | copy-start | bytes 100
  221.8 9.3 %copy-start.1 = (f32[32,32,64]{2,0,1:T(8,128)S(1)}, f32[32,32,64]{2,0,1:T(8,128)}, u32[]{:S(2)}) copy-start(f32[32,32,64]{2,0,1:T(8,128)} %convolution_bitcast_fusion.2) | copy-start | bytes 786436
  225.2 6.0 %copy-start.6 = (bf16[32,64,64]{2,1,0:T(8,128)(2,1)S(1)}, bf16[32,64,64]{2,1,0:T(8,128)(2,1)}, u32[]{:S(2)}) copy-start(bf16[32,64,64]{2,1,0:T(8,128)(2,1)} %param.23) | copy-start | bytes 786436
  227.0 13.1 %all-to-all-start = ((bf16[4,32,2048]{2,1,0:T(8,128)(2,1)}), bf16[4,32,2048]{2,1,0:T(8,128)(2,1)}, u32[]{:S(2)}, u32[]{:S(2)}) async-start(bf16[4,32,2048]{2,1,0:T(8,128)(2,1)} %pad_maximum_fusion.1), calls=%async_computation | async-start | bytes 1048576 | tf_op jit(solution)/shard_map/all_to_all | solution.py:15
Sparse Core Ops, SparseCore 0:
  63.3 49.5 all-gather.1
